TPU v7x, 32 devices: a whole 2x2x4 slice. The times are simulated.
32 devices in a mesh: gx: 4 (over x, core), gy: 8 (over z, y).
Axes of the slice: x: 2, y: 2, z: 4, core: 2. Of those that a mesh axis runs over, the one named last changes fastest.
Arguments:
- fine_nodes: bfloat16 [4, 8, 512, 128], P('gx', 'gy'), may hold values from -6 to 6
- fine_edges: int32 [4, 8, 2, 1536], P('gx', 'gy'), may hold values from 0 to 1023, as said below
- fine_live: int32 [4, 8], P('gx', 'gy'), may hold values from 512 to 1536, as said below
- fine_halo: int32 [4, 8, 4, 1], P('gx', 'gy'), may hold values from 0 to 3, as said below
- pool_map: int32 [4, 8, 512], P('gx', 'gy'), may hold values from 0 to 255, as said below
- coarse_edges: int32 [4, 8, 2, 2048], P('gx', 'gy'), may hold values from 0 to 767, as said below
- coarse_halo: int32 [4, 8, 4, 1], P('gx', 'gy'), may hold values from 0 to 1, as said below
- fine_weights: bfloat16 [5, 128, 128], replicated, may hold values from -0.5 to 0.5
- fine_bias: float32 [128], replicated, may hold values from -3 to 3
- fine_gain: float32 [128], replicated, may hold values from 0.25 to 1.75
- coarse_weights: bfloat16 [2, 5, 128, 128], replicated, may hold values from -0.5 to 0.5
- coarse_bias: float32 [2, 128], replicated, may hold values from -3 to 3
- coarse_gain: float32 [2, 128], replicated, may hold values from 0.25 to 1.75
- cotangent: bfloat16 [4, 8, 512, 128], P('gx', 'gy'), may hold values from -6 to 6
Outputs:
- fine_out: bfloat16 [4, 8, 512, 128], P('gx', 'gy')
- grad_fine_weights: float32 [5, 128, 128], replicated
- grad_fine_bias: float32 [128], replicated
- grad_fine_gain: float32 [128], replicated
- grad_coarse_weights: float32 [2, 5, 128, 128], replicated
- grad_coarse_bias: float32 [2, 128], replicated
- grad_coarse_gain: float32 [2, 128], replicated
- grad_pooled: float32 [4, 8, 256, 128], P('gx', 'gy')
Inputs may be any that keep to these rules, and one draw needn't show every extreme that they name: `fine_edges`: row 0 of each device's slots names senders: below 512 a node of the device, from 512 on a row of the four halo groups; row 1 names receivers among the device's 512 nodes. `fine_live`: A multiple of 512; in every draw some device has all 1536 slots live. `fine_halo`: block numbers of the device's fine nodes; within one device and direction they differ. `pool_map`: every coarse node of a device is named by at least one of its fine nodes. `coarse_edges`: row 0 names senders: below 256 a coarse node of the device, from 256 on a row of the four coarse halo groups; row 1 names receivers among the device's 256 coarse nodes. `coarse_halo`: block numbers of the device's coarse nodes.
All inputs are finite; a program needn't handle non-finite values.
Results may differ from a plain program's by a relative error of at most 0.009.
Values may be sent and summed in bfloat16 or wider, within the bound.
A program may use at most 64 MiB of HBM per device.

v0:
```python
import math

import jax
import jax.numpy as jnp
from jax import lax
from jax.sharding import PartitionSpec as P

BLOCK = 128
EDGE_BLOCK = 512
COARSE_STEPS = 2
NC_DEV = 256


EPSILON = 1e-05


def extended_2(x, sides, width):
    for axis, dim in sides:
        peers, length = (lax.axis_size(axis), x.shape[dim])
        up = [(i, (i + 1) % peers) for i in range(peers - 1)]
        down = [(j, i) for i, j in up]
        last = lax.slice_in_dim(x, length - width, length, axis=dim)
        initial = lax.slice_in_dim(x, 0, width, axis=dim)
        before = lax.ppermute(last, axis, up)
        after = lax.ppermute(initial, axis, down)
        x = jnp.concatenate([before, x, after], axis=dim)
    return x


def layer_norm(values):
    centred = values - jnp.mean(values, axis=-1, keepdims=True)
    spread = jnp.mean(centred * centred, axis=-1, keepdims=True)
    return centred * lax.rsqrt(spread + EPSILON)


def split_parts(values):
    high = values.astype(jnp.bfloat16)
    low = (values - high.astype(jnp.float32)).astype(jnp.bfloat16)
    return (high, low)


def contract_rows(left, right):
    high, low = split_parts(right)
    numbers = (((0,), (0,)), ((), ()))
    return lax.dot_general(
        left, high, numbers, preferred_element_type=jnp.float32
    ) + lax.dot_general(left, low, numbers, preferred_element_type=jnp.float32)


def times_transpose(left, weight):
    high, low = split_parts(left)
    numbers = (((1,), (1,)), ((), ()))
    return lax.dot_general(
        high, weight, numbers, preferred_element_type=jnp.float32
    ) + lax.dot_general(low, weight, numbers, preferred_element_type=jnp.float32)


def make_one_hot(pool_rows, coarse_count):
    return (pool_rows[:, None] == lax.iota(jnp.int32, coarse_count)[None, :]).astype(jnp.bfloat16)


def pick_blocks(node_rows, block_lists):
    features = node_rows.shape[-1]
    blocked = node_rows.reshape(-1, BLOCK, features)
    return blocked[block_lists].reshape(4, -1, features)


def put_blocks(returned, block_lists, row_count):
    features = returned.shape[-1]
    total = (
        jnp.zeros((row_count // BLOCK, BLOCK, features), jnp.float32)
        .at[block_lists.reshape(-1)]
        .add(returned)
    )
    return total.reshape(row_count, features)


def slot_block(edge_list, live_slots, first_slot, block_width):
    senders = lax.dynamic_slice_in_dim(edge_list[0], first_slot, block_width)
    receivers = lax.dynamic_slice_in_dim(edge_list[1], first_slot, block_width)
    weights_live = (first_slot + lax.iota(jnp.int32, block_width) < live_slots).astype(jnp.float32)
    return (senders, receivers, weights_live)


def dot(left, right):
    return jnp.dot(left, right, preferred_element_type=jnp.float32)


def dot_rows(left, right):
    return lax.dot_general(left, right, (((0,), (0,)), ((), ())), preferred_element_type=jnp.float32)


def pick_matrix(edge_list, live_slots, ext_count, own_count):
    live = lax.iota(jnp.int32, edge_list.shape[1]) < live_slots
    senders = jnp.where(live, edge_list[0], -1)
    receivers = jnp.where(live, edge_list[1], -1)
    return jnp.concatenate([make_one_hot(senders, ext_count), make_one_hot(receivers, own_count)], axis=1)


def step_forward(node_rows, halo_rows, picks, weights, edge_bias, norm_gain):
    extended = jnp.concatenate([node_rows, halo_rows], axis=0)
    ext_count = extended.shape[0]
    table = jnp.concatenate([dot(extended, weights[0]), dot(node_rows, weights[1]) + edge_bias], axis=0)
    pre_act = dot(picks, table.astype(jnp.bfloat16))
    gate = jax.nn.sigmoid(pre_act)
    hidden = (pre_act * gate).astype(jnp.bfloat16)
    slope = gate * (1.0 + pre_act * (1.0 - gate))
    high, low = split_parts(dot_rows(picks[:, ext_count:], hidden))
    agg_low = (dot(high, weights[2]) + dot(low, weights[2])).astype(jnp.bfloat16)
    node_pre = dot(node_rows, weights[3]) + dot(agg_low, weights[4])
    output = (node_rows.astype(jnp.float32) + norm_gain * layer_norm(node_pre)).astype(jnp.bfloat16)
    return (output, (extended, high, slope, agg_low, node_pre))


def step_backward(upstream, node_rows, saved_state, picks, weights, norm_gain, want_input):
    extended, high, slope, agg_low, node_pre = saved_state
    row_count, ext_count = node_rows.shape[0], extended.shape[0]
    normed, norm_back = jax.vjp(layer_norm, node_pre)
    grad_gain = jnp.sum(upstream * normed, axis=0)
    grad_pre = norm_back(upstream * norm_gain)[0]
    grad_agg = times_transpose(grad_pre, weights[4])
    grad_hidden = times_transpose(grad_agg, weights[2])
    grad_act = dot(picks[:, ext_count:], grad_hidden.astype(jnp.bfloat16)) * slope
    gathered = dot_rows(picks, grad_act.astype(jnp.bfloat16))
    grad_send, grad_recv = gathered[:ext_count], gathered[ext_count:]
    grad_bias = jnp.sum(grad_recv, axis=0)
    grad_weights = jnp.stack(
        [
            contract_rows(extended, grad_send),
            contract_rows(node_rows, grad_recv),
            contract_rows(high, grad_agg),
            contract_rows(node_rows, grad_pre),
            contract_rows(agg_low, grad_pre),
        ]
    )
    if not want_input:
        return ((grad_weights, grad_bias, grad_gain), None, None)
    grad_ext = times_transpose(grad_send, weights[0])
    grad_nodes = (
        upstream
        + times_transpose(grad_pre, weights[3])
        + times_transpose(grad_recv, weights[1])
        + grad_ext[:row_count]
    )
    return ((grad_weights, grad_bias, grad_gain), grad_nodes, grad_ext[row_count:])


def fine_exchange(node_rows, block_lists):
    sends = pick_blocks(node_rows, block_lists)
    across = extended_2(sends[0:2], (("gx", 0),), 1)
    along = extended_2(sends[2:4], (("gy", 0),), 1)
    return jnp.concatenate([across[0], across[3], along[0], along[3]], axis=0)


def coarse_exchange(node_rows, block_lists):
    sends = pick_blocks(node_rows, block_lists)
    across = extended_2(sends[0:2], (("gx", 0),), 1)
    along = extended_2(sends[2:4], (("gy", 0),), 1)
    return jnp.concatenate([across[0], across[3], along[0], along[3]], axis=0)


def coarse_return(halo_grads, block_lists, row_count):
    split = halo_grads.reshape(4, -1, halo_grads.shape[-1])
    across = extended_2(split[0:2].astype(jnp.bfloat16), (("gx", 0),), 1).astype(jnp.float32)
    along = extended_2(split[2:4].astype(jnp.bfloat16), (("gy", 0),), 1).astype(jnp.float32)
    returned = jnp.stack([across[0], across[3], along[0], along[3]])
    return put_blocks(returned, block_lists, row_count)


def body(
    fine_nodes,
    fine_edges,
    fine_live,
    fine_halo,
    pool_map,
    coarse_edges,
    coarse_halo,
    fine_weights,
    fine_bias,
    fine_gain,
    coarse_weights,
    coarse_bias,
    coarse_gain,
    cotangent,
):
    node_rows = fine_nodes[0, 0]
    edge_list = fine_edges[0, 0]
    live_slots = fine_live[0, 0]
    pool_rows = pool_map[0, 0]
    coarse_list = coarse_edges[0, 0]
    coarse_blocks = coarse_halo[0, 0]
    coarse_slots = coarse_list.shape[1]
    halo_rows = fine_exchange(node_rows, fine_halo[0, 0])
    fine_picks = pick_matrix(edge_list, live_slots, node_rows.shape[0] + halo_rows.shape[0], node_rows.shape[0])
    coarse_picks = pick_matrix(coarse_list, coarse_slots, NC_DEV + 4 * BLOCK, NC_DEV)
    fine_mid, fine_saved = step_forward(
        node_rows,
        halo_rows,
        fine_picks,
        fine_weights,
        fine_bias,
        fine_gain,
    )
    one_hot = make_one_hot(pool_rows, NC_DEV)
    pooled_sums = lax.dot_general(
        one_hot, fine_mid, (((0,), (0,)), ((), ())), preferred_element_type=jnp.float32
    )
    counts = jnp.sum(one_hot, axis=0, dtype=jnp.float32)
    current = (pooled_sums / counts[:, None]).astype(jnp.bfloat16)
    states = []
    for step_index in range(COARSE_STEPS):
        coarse_rows = coarse_exchange(current, coarse_blocks)
        following, saved_state = step_forward(
            current,
            coarse_rows,
            coarse_picks,
            coarse_weights[step_index],
            coarse_bias[step_index],
            coarse_gain[step_index],
        )
        states.append((current, saved_state))
        current = following
    lifted = jnp.dot(one_hot, current, preferred_element_type=jnp.float32)
    fine_out = (fine_mid.astype(jnp.float32) + lifted).astype(jnp.bfloat16)
    total_nodes = node_rows.shape[0] * lax.axis_size("gx") * lax.axis_size("gy")
    loss_scale = 1.0 / math.sqrt(total_nodes)
    direct = cotangent[0, 0].astype(jnp.float32) * loss_scale
    upstream = dot_rows(one_hot, cotangent[0, 0]) * loss_scale
    coarse_terms = [None] * COARSE_STEPS
    for step_index in reversed(range(COARSE_STEPS)):
        inputs_now, saved_state = states[step_index]
        step_terms, grad_nodes, grad_halo = step_backward(
            upstream,
            inputs_now,
            saved_state,
            coarse_picks,
            coarse_weights[step_index],
            coarse_gain[step_index],
            True,
        )
        upstream = grad_nodes + coarse_return(grad_halo, coarse_blocks, NC_DEV)
        coarse_terms[step_index] = step_terms
    grad_pooled = upstream * math.sqrt(total_nodes)
    coarse_stacked = (
        jnp.stack([entry[0] for entry in coarse_terms]),
        jnp.stack([entry[1] for entry in coarse_terms]),
        jnp.stack([entry[2] for entry in coarse_terms]),
    )
    fine_seed = direct + dot(one_hot, (upstream / counts[:, None]).astype(jnp.bfloat16))
    fine_terms = step_backward(
        fine_seed,
        node_rows,
        fine_saved,
        fine_picks,
        fine_weights,
        fine_gain,
        False,
    )[0]
    everything = lax.psum(
        (
            fine_terms[0],
            fine_terms[1],
            fine_terms[2],
            coarse_stacked[0],
            coarse_stacked[1],
            coarse_stacked[2],
        ),
        ("gx", "gy"),
    )
    fine_total = everything[0:3]
    coarse_total = everything[3:6]
    return (
        fine_out[None, None],
        fine_total[0],
        fine_total[1],
        fine_total[2],
        coarse_total[0],
        coarse_total[1],
        coarse_total[2],
        grad_pooled[None, None],
    )


def solution(mesh):
    return jax.shard_map(
        body,
        mesh=mesh,
        in_specs=(
            P("gx", "gy", None, None),
            P("gx", "gy", None, None),
            P("gx", "gy"),
            P("gx", "gy", None, None),
            P("gx", "gy", None),
            P("gx", "gy", None, None),
            P("gx", "gy", None, None),
            P(),
            P(),
            P(),
            P(),
            P(),
            P(),
            P("gx", "gy", None, None),
        ),
        out_specs=(
            P("gx", "gy", None, None),
            P(),
            P(),
            P(),
            P(),
            P(),
            P(),
            P("gx", "gy", None, None),
        ),
        check_vma=False,
    )
```

profile of v0, /device:TPU:0, one launch (start us, length us, event | category | flops | bytes accessed | tf_op | source)
XLA Modules:
  0.0 306.5 jit_solution(9734569044855837338)
XLA Ops:
  8.5 1.5 gather_fusion
  10.8 3.0 collective-permute-start
  14.5 1.4 collective-permute-start.1
  16.0 4.2 %collective-permute-start.2 = (bf16[1,128,128]{1,2,0:T(8,128)(2,1)S(1)}, bf16[1,128,128]{1,2,0:T(8,128)(2,1)S(1)}, u32[]{:S(2)}, u32[]{:S(2)}) collective-permute-start(bf16[1,128,128]{1,2,0:T(8,128)(2,1)S(1)} %copy.92), channel_id=1, source_target_pairs={{0,1},{1,2},{2,3},{3,4},{4,5},{5,6},{6,7},{8,9},{9,10},{10,11},{11... | collective-permute-start | bytes 98312 | tf_op jit(solution)/shard_map/ppermute | solution.py:24
  21.0 1.3 collective-permute-start.3
  22.3 1.0 copy.58
  23.3 1.4 slice_bitcast_fusion.9
  24.7 1.2 broadcast_multiply_fusion.3
  25.9 1.2 fusion.229
  27.1 0.8 slice_reduce_fusion.3
  29.2 1.4 iota_compare_fusion.1
  30.8 0.9 fusion.12
  32.3 1.2 iota_compare_fusion.3
  33.4 1.9 iota_compare_fusion
  38.9 2.3 fusion
  41.2 1.3 fusion.262
  45.5 3.4 %collective-permute-start.4 = (bf16[1,128,128]{2,1,0:T(8,128)(2,1)S(1)}, bf16[1,128,128]{2,1,0:T(8,128)(2,1)S(1)}, u32[]{:S(2)}, u32[]{:S(2)}) collective-permute-start(bf16[1,128,128]{2,1,0:T(8,128)(2,1)S(1)} %get-tuple-element.85), channel_id=1, source_target_pairs={{0,8},{8,16},{16,24},{1,9},{9,17},{17,25},{2,10},{10,18},{18,26},{... | collective-permute-start | bytes 98312 | tf_op jit(solution)/shard_map/ppermute | solution.py:24
  49.0 1.3 collective-permute-start.5
  50.3 4.3 %collective-permute-start.6 = (bf16[1,128,128]{2,1,0:T(8,128)(2,1)S(1)}, bf16[1,128,128]{2,1,0:T(8,128)(2,1)S(1)}, u32[]{:S(2)}, u32[]{:S(2)}) collective-permute-start(bf16[1,128,128]{2,1,0:T(8,128)(2,1)S(1)} %get-tuple-element.83), channel_id=1, source_target_pairs={{0,1},{1,2},{2,3},{3,4},{4,5},{5,6},{6,7},{8,9},{9,10},{10,11},{11... | collective-permute-start | bytes 98312 | tf_op jit(solution)/shard_map/ppermute | solution.py:24
  54.5 1.3 collective-permute-start.7
  56.0 0.8 fusion.26
  56.9 3.9 %collective-permute-done.7 = bf16[1,128,128]{2,1,0:T(8,128)(2,1)S(1)} collective-permute-done((bf16[1,128,128]{2,1,0:T(8,128)(2,1)S(1)}, bf16[1,128,128]{2,1,0:T(8,128)(2,1)S(1)}, u32[]{:S(2)}, u32[]{:S(2)}) %collective-permute-start.7) | collective-permute-done | bytes 32800 | tf_op jit(solution)/shard_map/ppermute | solution.py:25
  61.0 2.3 fusion.86
  63.3 1.1 fusion.264
  66.0 0.8 fusion.137
  66.8 1.3 gather_fusion.2
  68.2 0.8 fusion.258
  69.0 3.7 %collective-permute-start.8 = (bf16[1,128,128]{2,1,0:T(8,128)(2,1)S(1)}, bf16[1,128,128]{2,1,0:T(8,128)(2,1)S(1)}, u32[]{:S(2)}, u32[]{:S(2)}) collective-permute-start(bf16[1,128,128]{2,1,0:T(8,128)(2,1)S(1)} %get-tuple-element.81), channel_id=1, source_target_pairs={{0,8},{8,16},{16,24},{1,9},{9,17},{17,25},{2,10},{10,18},{18,26},{... | collective-permute-start | bytes 98312 | tf_op jit(solution)/shard_map/ppermute | solution.py:24
  72.7 1.3 collective-permute-start.9
  74.0 4.5 %collective-permute-start.10 = (bf16[1,128,128]{2,1,0:T(8,128)(2,1)S(1)}, bf16[1,128,128]{2,1,0:T(8,128)(2,1)S(1)}, u32[]{:S(2)}, u32[]{:S(2)}) collective-permute-start(bf16[1,128,128]{2,1,0:T(8,128)(2,1)S(1)} %get-tuple-element.79), channel_id=1, source_target_pairs={{0,1},{1,2},{2,3},{3,4},{4,5},{5,6},{6,7},{8,9},{9,10},{10,11},{11... | collective-permute-start | bytes 98312 | tf_op jit(solution)/shard_map/ppermute | solution.py:24
  78.5 1.5 collective-permute-start.11
  80.0 0.8 fusion.28
  80.9 3.4 %collective-permute-done.11 = bf16[1,128,128]{2,1,0:T(8,128)(2,1)S(1)} collective-permute-done((bf16[1,128,128]{2,1,0:T(8,128)(2,1)S(1)}, bf16[1,128,128]{2,1,0:T(8,128)(2,1)S(1)}, u32[]{:S(2)}, u32[]{:S(2)}) %collective-permute-start.11) | collective-permute-done | bytes 32800 | tf_op jit(solution)/shard_map/ppermute | solution.py:25
  84.5 2.3 fusion.90
  86.9 1.1 fusion.266
  88.8 0.9 multiply_reduce_fusion.3
  90.4 0.8 fusion.135
  91.7 0.8 fusion.30
  92.5 4.4 %fusion.11 = f32[1024,128]{1,0:T(8,128)S(1)} fusion(bf16[256,128]{1,0:T(8,128)(2,1)} %fusion.30, f32[2048,128]{1,0:T(8,128)} %copy-done.61, s32[2048]{0:T(1024)S(1)} %fusion.221, pred[2048,256]{1,0:T(32,128)(4,1)S(1)} %copy-done.10, pred[2048,768]{1,0:T(32,128)(4,1)} %iota_compare_fusion), kind=kOutput, calls=%fused_computation.25 | convolution fusion | flops 676069376 | bytes 3743744 | tf_op jit(solution)/shard_map/dot_general | solution.py:90
  100.5 0.8 fusion.24
  101.4 5.0 %collective-permute-start.12 = (bf16[1,128,128]{2,1,0:T(8,128)(2,1)}, bf16[1,128,128]{2,1,0:T(8,128)(2,1)}, u32[]{:S(2)}, u32[]{:S(2)}) collective-permute-start(bf16[1,128,128]{2,1,0:T(8,128)(2,1)} %get-tuple-element.64), channel_id=1, source_target_pairs={{0,8},{8,16},{16,24},{1,9},{9,17},{17,25},{2,10},{10,18},{18,26},{... | collective-permute-start | bytes 98312 | tf_op jit(solution)/shard_map/ppermute | solution.py:24
  106.4 1.3 collective-permute-start.13
  107.6 3.8 %collective-permute-start.14 = (bf16[1,128,128]{2,1,0:T(8,128)(2,1)}, bf16[1,128,128]{2,1,0:T(8,128)(2,1)}, u32[]{:S(2)}, u32[]{:S(2)}) collective-permute-start(bf16[1,128,128]{2,1,0:T(8,128)(2,1)} %get-tuple-element.66), channel_id=1, source_target_pairs={{0,1},{1,2},{2,3},{3,4},{4,5},{5,6},{6,7},{8,9},{9,10},{10,11},{11... | collective-permute-start | bytes 98312 | tf_op jit(solution)/shard_map/ppermute | solution.py:24
  111.5 1.5 collective-permute-start.15
  116.8 0.8 collective-permute-done.15
  118.4 0.9 scatter_fusion
  119.3 1.4 multiply_reduce_fusion.4
  121.4 0.9 fusion.254
  123.3 4.6 %fusion.10 = f32[1024,128]{1,0:T(8,128)S(1)} fusion(bf16[256,128]{1,0:T(8,128)(2,1)S(1)} %fusion.31, f32[2048,128]{1,0:T(8,128)} %copy-done.60, s32[2048]{0:T(1024)S(1)} %fusion.221, pred[2048,256]{1,0:T(32,128)(4,1)} %iota_compare_fusion.3, pred[2048,768]{1,0:T(32,128)(4,1)} %iota_compare_fusion), kind=kOutput, calls=%fused_computation.24 | convolution fusion | flops 676069376 | bytes 3743744 | tf_op jit(solution)/shard_map/dot_general | solution.py:90
  129.9 3.7 %collective-permute-start.16 = (bf16[1,128,128]{2,1,0:T(8,128)(2,1)S(1)}, bf16[1,128,128]{2,1,0:T(8,128)(2,1)S(1)}, u32[]{:S(2)}, u32[]{:S(2)}) collective-permute-start(bf16[1,128,128]{2,1,0:T(8,128)(2,1)S(1)} %get-tuple-element.58), channel_id=1, source_target_pairs={{0,8},{8,16},{16,24},{1,9},{9,17},{17,25},{2,10},{10,18},{18,26},{... | collective-permute-start | bytes 98312 | tf_op jit(solution)/shard_map/ppermute | solution.py:24
  133.7 1.3 collective-permute-start.17
  136.1 0.9 pad_maximum_fusion
  137.0 4.4 %collective-permute-start.18 = (bf16[1,128,128]{2,1,0:T(8,128)(2,1)S(1)}, bf16[1,128,128]{2,1,0:T(8,128)(2,1)S(1)}, u32[]{:S(2)}, u32[]{:S(2)}) collective-permute-start(bf16[1,128,128]{2,1,0:T(8,128)(2,1)S(1)} %get-tuple-element.60), channel_id=1, source_target_pairs={{0,1},{1,2},{2,3},{3,4},{4,5},{5,6},{6,7},{8,9},{9,10},{10,11},{11... | collective-permute-start | bytes 98312 | tf_op jit(solution)/shard_map/ppermute | solution.py:24
  141.4 1.3 collective-permute-start.19
  143.0 4.5 %collective-permute-done.19 = bf16[1,128,128]{2,1,0:T(8,128)(2,1)S(1)} collective-permute-done((bf16[1,128,128]{2,1,0:T(8,128)(2,1)S(1)}, bf16[1,128,128]{2,1,0:T(8,128)(2,1)S(1)}, u32[]{:S(2)}, u32[]{:S(2)}) %collective-permute-start.19) | collective-permute-done | bytes 32800 | tf_op jit(solution)/shard_map/ppermute | solution.py:25
  149.5 0.9 fusion.219
  150.4 0.9 fusion.100
  151.6 0.9 fusion.235
  152.5 3.0 fusion.4
  155.5 3.9 %fusion.1 = f32[1536,128]{1,0:T(8,128)S(1)} fusion(bf16[1536,128]{1,0:T(8,128)(2,1)} %fusion.4, pred[1536,512]{1,0:T(32,128)(4,1)} %copy-done.7, pred[1536,1024]{1,0:T(32,128)(4,1)S(1)} %copy-done.3), kind=kOutput, calls=%fused_computation.11 | convolution fusion | flops 606339072 | bytes 3538944 | tf_op jit(solution)/shard_map/dot_general | solution.py:90
  161.9 45.0 %all-reduce = (f32[128]{0:T(128)}, f32[128]{0:T(128)}, f32[2,128]{1,0:T(2,128)}, f32[2,128]{1,0:T(2,128)}) all-reduce(f32[128]{0:T(128)S(1)} %slice_reduce_fusion, f32[128]{0:T(128)S(1)} %get-tuple-element.32, f32[2,128]{1,0:T(2,128)S(1)} %pad_maximum_fusion.11, ...), channel_id=1, replica_groups=mesh['gx'=4,'gy'=8] {'gx','gy'}, use_global_device_ids=true, to_apply=%region_17.18 | all-reduce | flops 768 | bytes 6144 | tf_op jit(solution)/shard_map/psum | solution.py:259
  207.6 88.4 %all-reduce.4.cloned.1.call-done = (f32[5,128,128]{2,1,0:T(8,128)}, f32[2,5,128,128]{3,2,1,0:T(8,128)}) async-done(((f32[5,128,128]{2,1,0:T(8,128)}, f32[2,5,128,128]{3,2,1,0:T(8,128)}), (f32[5,128,128]{2,1,0:T(8,128)}, f32[2,5,128,128]{3,2,1,0:T(8,128)})) %all-reduce.4.cloned.1.call-update) | async-done | bytes 983056 | tf_op jit(solution)/shard_map/psum | solution.py:259
  296.0 1.7 copy.139
  297.7 2.0 copy.140
  (278 shorter events, 33.8 us)
Async XLA Ops:
  7.2 288.8 %all-reduce.4.cloned.1.call-start = ((), (), s32[]{:S(2)}) async-start(), calls=%async_computation | async-start | bytes 1966080 | tf_op jit(solution)/shard_map/psum | solution.py:259
  8.5 36.4 %copy-start.40 = (s32[1024]{0:T(1024)}, s32[1024]{0:T(1024)S(1)}, u32[]{:S(2)}) copy-start(s32[1024]{0:T(1024)S(1)} %get-tuple-element.119) | copy-start | bytes 12292
  10.8 25.5 %collective-permute-start = (bf16[1,128,128]{1,2,0:T(8,128)(2,1)}, bf16[1,128,128]{1,2,0:T(8,128)(2,1)}, u32[]{:S(2)}, u32[]{:S(2)}) collective-permute-start(bf16[1,128,128]{1,2,0:T(8,128)(2,1)} %copy.90), channel_id=1, source_target_pairs={{0,8},{8,16},{16,24},{1,9},{9,17},{17,25},{2,10},{10,18},{18,26},{... | collective-permute-start | bytes 98312 | tf_op jit(solution)/shard_map/ppermute | solution.py:24
  14.5 16.0 %copy-start = (bf16[1,1,512,128]{3,2,1,0:T(8,128)(2,1)S(1)}, bf16[1,1,512,128]{3,2,1,0:T(8,128)(2,1)}, u32[]{:S(2)}) copy-start(bf16[1,1,512,128]{3,2,1,0:T(8,128)(2,1)} %param.14) | copy-start | bytes 393220
  14.5 16.0 %copy-start.8 = (bf16[5,128,128]{2,1,0:T(8,128)(2,1)S(1)}, bf16[5,128,128]{2,1,0:T(8,128)(2,1)}, u32[]{:S(2)}) copy-start(bf16[5,128,128]{2,1,0:T(8,128)(2,1)} %param.21) | copy-start | bytes 491524
  14.5 22.6 %collective-permute-start.1 = (bf16[1,128,128]{1,2,0:T(8,128)(2,1)}, bf16[1,128,128]{1,2,0:T(8,128)(2,1)}, u32[]{:S(2)}, u32[]{:S(2)}) collective-permute-start(bf16[1,128,128]{1,2,0:T(8,128)(2,1)} %copy.91), channel_id=1, source_target_pairs={{8,0},{16,8},{24,16},{9,1},{17,9},{25,17},{10,2},{18,10},{26,18},{... | collective-permute-start | bytes 98312 | tf_op jit(solution)/shard_map/ppermute | solution.py:25
  16.0 21.8 %collective-permute-start.2 = (bf16[1,128,128]{1,2,0:T(8,128)(2,1)S(1)}, bf16[1,128,128]{1,2,0:T(8,128)(2,1)S(1)}, u32[]{:S(2)}, u32[]{:S(2)}) collective-permute-start(bf16[1,128,128]{1,2,0:T(8,128)(2,1)S(1)} %copy.92), channel_id=1, source_target_pairs={{0,1},{1,2},{2,3},{3,4},{4,5},{5,6},{6,7},{8,9},{9,10},{10,11},{11... | collective-permute-start | bytes 98312 | tf_op jit(solution)/shard_map/ppermute | solution.py:24
  21.0 16.8 %collective-permute-start.3 = (bf16[1,128,128]{1,2,0:T(8,128)(2,1)}, bf16[1,128,128]{1,2,0:T(8,128)(2,1)}, u32[]{:S(2)}, u32[]{:S(2)}) collective-permute-start(bf16[1,128,128]{1,2,0:T(8,128)(2,1)} %copy.93), channel_id=1, source_target_pairs={{1,0},{2,1},{3,2},{4,3},{5,4},{6,5},{7,6},{9,8},{10,9},{11,10},{12... | collective-permute-start | bytes 98312 | tf_op jit(solution)/shard_map/ppermute | solution.py:25
  23.3 7.5 %copy-start.55 = (f32[128]{0:T(128)S(1)}, f32[128]{0:T(128)}, u32[]{:S(2)}) copy-start(f32[128]{0:T(128)} %param.22) | copy-start | bytes 1540
  27.9 3.8 %copy-start.54 = (f32[2,128]{1,0:T(2,128)S(1)}, f32[2,128]{1,0:T(2,128)}, u32[]{:S(2)}) copy-start(f32[2,128]{1,0:T(2,128)} %param.25) | copy-start | bytes 3076
  27.9 4.3 %copy-start.34 = (s32[1,1,2,2048]{3,2,1,0:T(2,128)S(1)}, s32[1,1,2,2048]{3,2,1,0:T(2,128)}, u32[]{:S(2)}) copy-start(s32[1,1,2,2048]{3,2,1,0:T(2,128)} %param.19) | copy-start | bytes 49156
  28.6 12.6 %copy-start.28 = (s32[1536]{0:T(1024)}, s32[1536]{0:T(1024)S(1)}, u32[]{:S(2)}) copy-start(s32[1536]{0:T(1024)S(1)} %get-tuple-element.118) | copy-start | bytes 18436
  29.1 9.7 %copy-start.7 = (pred[1536,512]{1,0:T(32,128)(4,1)}, pred[1536,512]{1,0:T(32,128)(4,1)S(1)}, u32[]{:S(2)}) copy-start(pred[1536,512]{1,0:T(32,128)(4,1)S(1)} %iota_compare_fusion.2) | copy-start | bytes 2359300
  30.5 8.4 %copy-start.2 = (pred[1536,1024]{1,0:T(32,128)(4,1)}, pred[1536,1024]{1,0:T(32,128)(4,1)S(1)}, u32[]{:S(2)}) copy-start(pred[1536,1024]{1,0:T(32,128)(4,1)S(1)} %iota_compare_fusion.1) | copy-start | bytes 4718596
  30.5 4.8 %copy-start.45 = (s32[1,1,512]{2,1,0:T(1,128)S(1)}, s32[1,1,512]{2,1,0:T(1,128)}, u32[]{:S(2)}) copy-start(s32[1,1,512]{2,1,0:T(1,128)} %param.18) | copy-start | bytes 6148
  30.6 4.9 %copy-start.25 = (bf16[1,1,512,128]{3,2,1,0:T(8,128)(2,1)S(1)}, bf16[1,1,512,128]{3,2,1,0:T(8,128)(2,1)}, u32[]{:S(2)}) copy-start(bf16[1,1,512,128]{3,2,1,0:T(8,128)(2,1)} %param.27) | copy-start | bytes 393220
  35.5 9.0 %copy-start.52 = (f32[256]{0:T(256)}, f32[256]{0:T(256)S(1)}, u32[]{:S(2)}) copy-start(f32[256]{0:T(256)S(1)} %convert_reduce_fusion) | copy-start | bytes 3076
  42.5 1.9 copy-start.49
  42.9 13.0 %copy-start.1 = (bf16[2,5,128,128]{3,2,1,0:T(8,128)(2,1)S(1)}, bf16[2,5,128,128]{3,2,1,0:T(8,128)(2,1)}, u32[]{:S(2)}) copy-start(bf16[2,5,128,128]{3,2,1,0:T(8,128)(2,1)} %param.24) | copy-start | bytes 983044
  43.8 17.2 %copy-start.4 = (pred[2048,768]{1,0:T(32,128)(4,1)S(1)}, pred[2048,768]{1,0:T(32,128)(4,1)}, u32[]{:S(2)}) copy-start(pred[2048,768]{1,0:T(32,128)(4,1)} %iota_compare_fusion) | copy-start | bytes 4718596
  44.5 18.8 %copy-start.23 = (bf16[512,128]{0,1:T(8,128)(2,1)}, bf16[512,128]{0,1:T(8,128)(2,1)S(1)}, u32[]{:S(2)}) copy-start(bf16[512,128]{0,1:T(8,128)(2,1)S(1)} %add_convert_fusion) | copy-start | bytes 393220
  45.5 11.3 %collective-permute-start.4 = (bf16[1,128,128]{2,1,0:T(8,128)(2,1)S(1)}, bf16[1,128,128]{2,1,0:T(8,128)(2,1)S(1)}, u32[]{:S(2)}, u32[]{:S(2)}) collective-permute-start(bf16[1,128,128]{2,1,0:T(8,128)(2,1)S(1)} %get-tuple-element.85), channel_id=1, source_target_pairs={{0,8},{8,16},{16,24},{1,9},{9,17},{17,25},{2,10},{10,18},{18,26},{... | collective-permute-start | bytes 98312 | tf_op jit(solution)/shard_map/ppermute | solution.py:24
  49.0 7.9 %collective-permute-start.5 = (bf16[1,128,128]{2,1,0:T(8,128)(2,1)S(1)}, bf16[1,128,128]{2,1,0:T(8,128)(2,1)S(1)}, u32[]{:S(2)}, u32[]{:S(2)}) collective-permute-start(bf16[1,128,128]{2,1,0:T(8,128)(2,1)S(1)} %get-tuple-element.84), channel_id=1, source_target_pairs={{8,0},{16,8},{24,16},{9,1},{17,9},{25,17},{10,2},{18,10},{26,18},{... | collective-permute-start | bytes 98312 | tf_op jit(solution)/shard_map/ppermute | solution.py:25
  50.3 6.6 %collective-permute-start.6 = (bf16[1,128,128]{2,1,0:T(8,128)(2,1)S(1)}, bf16[1,128,128]{2,1,0:T(8,128)(2,1)S(1)}, u32[]{:S(2)}, u32[]{:S(2)}) collective-permute-start(bf16[1,128,128]{2,1,0:T(8,128)(2,1)S(1)} %get-tuple-element.83), channel_id=1, source_target_pairs={{0,1},{1,2},{2,3},{3,4},{4,5},{5,6},{6,7},{8,9},{9,10},{10,11},{11... | collective-permute-start | bytes 98312 | tf_op jit(solution)/shard_map/ppermute | solution.py:24
  54.5 6.2 %collective-permute-start.7 = (bf16[1,128,128]{2,1,0:T(8,128)(2,1)S(1)}, bf16[1,128,128]{2,1,0:T(8,128)(2,1)S(1)}, u32[]{:S(2)}, u32[]{:S(2)}) collective-permute-start(bf16[1,128,128]{2,1,0:T(8,128)(2,1)S(1)} %get-tuple-element.82), channel_id=1, source_target_pairs={{1,0},{2,1},{3,2},{4,3},{5,4},{6,5},{7,6},{9,8},{10,9},{11,10},{12... | collective-permute-start | bytes 98312 | tf_op jit(solution)/shard_map/ppermute | solution.py:25
  63.3 2.5 copy-start.39
  69.0 11.8 %collective-permute-start.8 = (bf16[1,128,128]{2,1,0:T(8,128)(2,1)S(1)}, bf16[1,128,128]{2,1,0:T(8,128)(2,1)S(1)}, u32[]{:S(2)}, u32[]{:S(2)}) collective-permute-start(bf16[1,128,128]{2,1,0:T(8,128)(2,1)S(1)} %get-tuple-element.81), channel_id=1, source_target_pairs={{0,8},{8,16},{16,24},{1,9},{9,17},{17,25},{2,10},{10,18},{18,26},{... | collective-permute-start | bytes 98312 | tf_op jit(solution)/shard_map/ppermute | solution.py:24
  72.7 8.2 %collective-permute-start.9 = (bf16[1,128,128]{2,1,0:T(8,128)(2,1)S(1)}, bf16[1,128,128]{2,1,0:T(8,128)(2,1)S(1)}, u32[]{:S(2)}, u32[]{:S(2)}) collective-permute-start(bf16[1,128,128]{2,1,0:T(8,128)(2,1)S(1)} %get-tuple-element.80), channel_id=1, source_target_pairs={{8,0},{16,8},{24,16},{9,1},{17,9},{25,17},{10,2},{18,10},{26,18},{... | collective-permute-start | bytes 98312 | tf_op jit(solution)/shard_map/ppermute | solution.py:25
  74.0 6.9 %collective-permute-start.10 = (bf16[1,128,128]{2,1,0:T(8,128)(2,1)S(1)}, bf16[1,128,128]{2,1,0:T(8,128)(2,1)S(1)}, u32[]{:S(2)}, u32[]{:S(2)}) collective-permute-start(bf16[1,128,128]{2,1,0:T(8,128)(2,1)S(1)} %get-tuple-element.79), channel_id=1, source_target_pairs={{0,1},{1,2},{2,3},{3,4},{4,5},{5,6},{6,7},{8,9},{9,10},{10,11},{11... | collective-permute-start | bytes 98312 | tf_op jit(solution)/shard_map/ppermute | solution.py:24
  78.5 5.8 %collective-permute-start.11 = (bf16[1,128,128]{2,1,0:T(8,128)(2,1)S(1)}, bf16[1,128,128]{2,1,0:T(8,128)(2,1)S(1)}, u32[]{:S(2)}, u32[]{:S(2)}) collective-permute-start(bf16[1,128,128]{2,1,0:T(8,128)(2,1)S(1)} %get-tuple-element.78), channel_id=1, source_target_pairs={{1,0},{2,1},{3,2},{4,3},{5,4},{6,5},{7,6},{9,8},{10,9},{11,10},{12... | collective-permute-start | bytes 98312 | tf_op jit(solution)/shard_map/ppermute | solution.py:25
  86.9 1.9 copy-start.26
  86.9 1.9 copy-start.46
  86.9 1.9 copy-start.56
  88.3 4.2 %copy-start.10 = (pred[2048,256]{1,0:T(32,128)(4,1)S(1)}, pred[2048,256]{1,0:T(32,128)(4,1)}, u32[]{:S(2)}) copy-start(pred[2048,256]{1,0:T(32,128)(4,1)} %iota_compare_fusion.3) | copy-start | bytes 1572868
  97.3 3.2 %copy-start.12 = (f32[256,128]{1,0:T(8,128)S(1)}, f32[256,128]{1,0:T(8,128)}, u32[]{:S(2)}) copy-start(f32[256,128]{1,0:T(8,128)} %fusion.135) | copy-start | bytes 393220
  97.4 3.2 %copy-start.14 = (f32[256,128]{1,0:T(8,128)S(1)}, f32[256,128]{1,0:T(8,128)}, u32[]{:S(2)}) copy-start(f32[256,128]{1,0:T(8,128)} %copy-done.13) | copy-start | bytes 393220
  100.0 14.8 %copy-start.24 = (bf16[512,128]{0,1:T(8,128)(2,1)S(1)}, bf16[512,128]{0,1:T(8,128)(2,1)}, u32[]{:S(2)}) copy-start(bf16[512,128]{0,1:T(8,128)(2,1)} %copy-done.23) | copy-start | bytes 393220
  100.0 14.8 %copy-start.37 = (f32[256]{0:T(256)S(1)}, f32[256]{0:T(256)}, u32[]{:S(2)}) copy-start(f32[256]{0:T(256)} %copy-done.36) | copy-start | bytes 3076
  100.0 14.7 %copy-start.42 = (f32[256]{0:T(256)S(1)}, f32[256]{0:T(256)}, u32[]{:S(2)}) copy-start(f32[256]{0:T(256)} %copy-done.41) | copy-start | bytes 3076
  100.0 14.7 %copy-start.47 = (s32[1,1,512]{2,1,0:T(1,128)S(1)}, s32[1,1,512]{2,1,0:T(1,128)}, u32[]{:S(2)}) copy-start(s32[1,1,512]{2,1,0:T(1,128)} %param.18) | copy-start | bytes 6148
  100.1 14.7 %copy-start.58 = (f32[128]{0:T(128)S(1)}, f32[128]{0:T(128)}, u32[]{:S(2)}) copy-start(f32[128]{0:T(128)} %get-tuple-element.92) | copy-start | bytes 1540
  101.4 16.2 %copy-start.21 = (bf16[256,128]{1,0:T(8,128)(2,1)S(1)}, bf16[256,128]{1,0:T(8,128)(2,1)}, u32[]{:S(2)}) copy-start(bf16[256,128]{1,0:T(8,128)(2,1)} %get-tuple-element.69) | copy-start | bytes 196612
  101.4 14.6 %collective-permute-start.12 = (bf16[1,128,128]{2,1,0:T(8,128)(2,1)}, bf16[1,128,128]{2,1,0:T(8,128)(2,1)}, u32[]{:S(2)}, u32[]{:S(2)}) collective-permute-start(bf16[1,128,128]{2,1,0:T(8,128)(2,1)} %get-tuple-element.64), channel_id=1, source_target_pairs={{0,8},{8,16},{16,24},{1,9},{9,17},{17,25},{2,10},{10,18},{18,26},{... | collective-permute-start | bytes 98312 | tf_op jit(solution)/shard_map/ppermute | solution.py:24
  106.4 9.6 %collective-permute-start.13 = (bf16[1,128,128]{2,1,0:T(8,128)(2,1)}, bf16[1,128,128]{2,1,0:T(8,128)(2,1)}, u32[]{:S(2)}, u32[]{:S(2)}) collective-permute-start(bf16[1,128,128]{2,1,0:T(8,128)(2,1)} %get-tuple-element.67), channel_id=1, source_target_pairs={{8,0},{16,8},{24,16},{9,1},{17,9},{25,17},{10,2},{18,10},{26,18},{... | collective-permute-start | bytes 98312 | tf_op jit(solution)/shard_map/ppermute | solution.py:25
  107.6 9.1 %collective-permute-start.14 = (bf16[1,128,128]{2,1,0:T(8,128)(2,1)}, bf16[1,128,128]{2,1,0:T(8,128)(2,1)}, u32[]{:S(2)}, u32[]{:S(2)}) collective-permute-start(bf16[1,128,128]{2,1,0:T(8,128)(2,1)} %get-tuple-element.66), channel_id=1, source_target_pairs={{0,1},{1,2},{2,3},{3,4},{4,5},{5,6},{6,7},{8,9},{9,10},{10,11},{11... | collective-permute-start | bytes 98312 | tf_op jit(solution)/shard_map/ppermute | solution.py:24
  111.5 6.1 %collective-permute-start.15 = (bf16[1,128,128]{2,1,0:T(8,128)(2,1)}, bf16[1,128,128]{2,1,0:T(8,128)(2,1)}, u32[]{:S(2)}, u32[]{:S(2)}) collective-permute-start(bf16[1,128,128]{2,1,0:T(8,128)(2,1)} %get-tuple-element.65), channel_id=1, source_target_pairs={{1,0},{2,1},{3,2},{4,3},{5,4},{6,5},{7,6},{9,8},{10,9},{11,10},{12... | collective-permute-start | bytes 98312 | tf_op jit(solution)/shard_map/ppermute | solution.py:25
  113.8 5.5 %copy-start.15 = (f32[256,128]{1,0:T(8,128)S(1)}, f32[256,128]{1,0:T(8,128)}, u32[]{:S(2)}) copy-start(f32[256,128]{1,0:T(8,128)} %fusion.24) | copy-start | bytes 393220
  129.3 6.7 %copy-start.17 = (f32[5,128,128]{2,1,0:T(8,128)S(1)}, f32[5,128,128]{2,1,0:T(8,128)}, u32[]{:S(2)}) copy-start(f32[5,128,128]{2,1,0:T(8,128)} %copy-done.16) | copy-start | bytes 983044
  129.9 12.8 %collective-permute-start.16 = (bf16[1,128,128]{2,1,0:T(8,128)(2,1)S(1)}, bf16[1,128,128]{2,1,0:T(8,128)(2,1)S(1)}, u32[]{:S(2)}, u32[]{:S(2)}) collective-permute-start(bf16[1,128,128]{2,1,0:T(8,128)(2,1)S(1)} %get-tuple-element.58), channel_id=1, source_target_pairs={{0,8},{8,16},{16,24},{1,9},{9,17},{17,25},{2,10},{10,18},{18,26},{... | collective-permute-start | bytes 98312 | tf_op jit(solution)/shard_map/ppermute | solution.py:24
  133.7 9.0 %collective-permute-start.17 = (bf16[1,128,128]{2,1,0:T(8,128)(2,1)S(1)}, bf16[1,128,128]{2,1,0:T(8,128)(2,1)S(1)}, u32[]{:S(2)}, u32[]{:S(2)}) collective-permute-start(bf16[1,128,128]{2,1,0:T(8,128)(2,1)S(1)} %get-tuple-element.61), channel_id=1, source_target_pairs={{8,0},{16,8},{24,16},{9,1},{17,9},{25,17},{10,2},{18,10},{26,18},{... | collective-permute-start | bytes 98312 | tf_op jit(solution)/shard_map/ppermute | solution.py:25
  135.6 12.0 %copy-start.51 = (s32[4]{0:T(128)S(1)}, s32[4]{0:T(128)}, u32[]{:S(2)}) copy-start(s32[4]{0:T(128)} %fusion.229) | copy-start | bytes 52
  136.9 11.6 %copy-start.27 = (bf16[1,1,512,128]{2,3,1,0:T(8,128)(2,1)S(1)}, bf16[1,1,512,128]{2,3,1,0:T(8,128)(2,1)}, u32[]{:S(2)}) copy-start(bf16[1,1,512,128]{2,3,1,0:T(8,128)(2,1)} %copy.66) | copy-start | bytes 393220
  136.9 11.6 %copy-start.31 = (f32[512]{0:T(512)S(1)}, f32[512]{0:T(512)}, u32[]{:S(2)}) copy-start(f32[512]{0:T(512)} %copy-done.30) | copy-start | bytes 6148
  136.9 11.6 %copy-start.48 = (s32[1,1,512]{2,1,0:T(1,128)S(1)}, s32[1,1,512]{2,1,0:T(1,128)}, u32[]{:S(2)}) copy-start(s32[1,1,512]{2,1,0:T(1,128)} %param.18) | copy-start | bytes 6148
  136.9 11.6 %copy-start.50 = (f32[128]{0:T(128)S(1)}, f32[128]{0:T(128)}, u32[]{:S(2)}) copy-start(f32[128]{0:T(128)} %param.23) | copy-start | bytes 1540
  137.0 11.7 %copy-start.53 = (f32[256]{0:T(256)S(1)}, f32[256]{0:T(256)}, u32[]{:S(2)}) copy-start(f32[256]{0:T(256)} %copy-done.52) | copy-start | bytes 3076
  137.0 6.0 %collective-permute-start.18 = (bf16[1,128,128]{2,1,0:T(8,128)(2,1)S(1)}, bf16[1,128,128]{2,1,0:T(8,128)(2,1)S(1)}, u32[]{:S(2)}, u32[]{:S(2)}) collective-permute-start(bf16[1,128,128]{2,1,0:T(8,128)(2,1)S(1)} %get-tuple-element.60), channel_id=1, source_target_pairs={{0,1},{1,2},{2,3},{3,4},{4,5},{5,6},{6,7},{8,9},{9,10},{10,11},{11... | collective-permute-start | bytes 98312 | tf_op jit(solution)/shard_map/ppermute | solution.py:24
  141.4 6.1 %collective-permute-start.19 = (bf16[1,128,128]{2,1,0:T(8,128)(2,1)S(1)}, bf16[1,128,128]{2,1,0:T(8,128)(2,1)S(1)}, u32[]{:S(2)}, u32[]{:S(2)}) collective-permute-start(bf16[1,128,128]{2,1,0:T(8,128)(2,1)S(1)} %get-tuple-element.59), channel_id=1, source_target_pairs={{1,0},{2,1},{3,2},{4,3},{5,4},{6,5},{7,6},{9,8},{10,9},{11,10},{12... | collective-permute-start | bytes 98312 | tf_op jit(solution)/shard_map/ppermute | solution.py:25
  147.6 1.5 copy-start.33
  149.3 3.2 %copy-start.29 = (s32[1536]{0:T(1024)S(1)}, s32[1536]{0:T(1024)}, u32[]{:S(2)}) copy-start(s32[1536]{0:T(1024)} %copy-done.28) | copy-start | bytes 18436
  152.5 3.0 copy-start.3
  160.0 1.8 copy-start.44
  160.1 1.8 copy-start.57
  160.1 1.8 copy-start.43
  (19 other events, 18.0 us)
Sparse Core Ops, SparseCore 0:
  161.9 134.0 all-reduce.3
where the time goes:
time: 308 us; the launch traced here: 307 us
  waiting for transfers between devices  101 us (33%)
  starting transfers between devices  53.6 us (17%)
  matrix products  49.7 us (16%)
  blocking collectives  45 us (15%)
  local copies, waits for them, and re-layouts  23.3 us (8%)
  other arithmetic  17.3 us (6%)
  between operations  16.3 us (5%)
    psum x1, waiting for transfers between devices, body(): lax.psum((fine_terms[0], fine_terms[1], fine_terms[2], coarse_stacked[0],...  88.4 us
    psum x1, blocking collectives, body(): lax.psum((fine_terms[0], fine_terms[1], fine_terms[2], coarse_stacked[0],...  45 us
    ppermute x10, starting transfers between devices, extended_2(): before = lax.ppermute(last, axis, up)  40.1 us
    dot_general x7, matrix products, dot_rows(): lax.dot_general(left, right, (((0,), (0,)), ((), ())), preferred_element_...  17.1 us
    dot_general x23, matrix products, dot(): return jnp.dot(left, right, preferred_element_type=jnp.float32)  16.3 us
    unnamed x143, local copies, waits for them, and re-layouts  14.2 us
    ppermute x10, starting transfers between devices, extended_2(): after = lax.ppermute(initial, axis, down)  13.4 us
    ppermute x10, waiting for transfers between devices, extended_2(): after = lax.ppermute(initial, axis, down)  12.7 us
  transfers between devices with their start and end apart: 21, of which 6 were waited for; matrix products, arithmetic and copies ran while one was open for 8% of the time, Pallas kernels for 0%

commit v1 on v0

v1 whole, which is shorter than its diff:
```python
import functools
import math

import jax
import jax.numpy as jnp
from jax import lax
from jax.experimental import pallas as pl
from jax.experimental.pallas import tpu as pltpu
from jax.sharding import PartitionSpec as P

BLOCK = 128
NC_DEV = 256
LANES = 128
EPSILON = 1e-05
MESH = pl.DeviceIdType.MESH
BF = jnp.bfloat16
F32 = jnp.float32
ROWS = 512


def dot(a, b):
    return lax.dot_general(a, b, (((1,), (0,)), ((), ())), preferred_element_type=F32)


def dot_t(a, b):
    return lax.dot_general(a, b, (((1,), (1,)), ((), ())), preferred_element_type=F32)


def dot_rows(a, b):
    return lax.dot_general(a, b, (((0,), (0,)), ((), ())), preferred_element_type=F32)


def parts(values):
    high = values.astype(BF)
    low = (values - high.astype(F32)).astype(BF)
    return high, low


def side(*pieces):
    return jnp.concatenate(pieces, axis=1)


def halves(values):
    width = values.shape[1] // 2
    return values[:, :width] + values[:, width:]


def times_t(left, weight):
    return dot_t(side(*parts(left)), side(weight, weight))


def norm(values):
    centred = values - jnp.mean(values, axis=-1, keepdims=True)
    spread = jnp.mean(centred * centred, axis=-1, keepdims=True)
    scale = lax.rsqrt(spread + EPSILON)
    return centred * scale, scale


def norm_back(grad, normed, scale):
    first = jnp.mean(grad, axis=-1, keepdims=True)
    second = jnp.mean(grad * normed, axis=-1, keepdims=True)
    return scale * (grad - first - normed * second)


def round_up(value, step):
    return (value + step - 1) // step * step


def marks(offsets, start):
    return jnp.where(offsets == start, 1.0, 0.0).astype(BF)


def step_kernel(nx, ny, loss_scale, out_scale, group_rows, fnodes, fedges, flive, fhalo_list, pool, cedges, chalo_list,
                fw, fb, fg, cw, cb, cg, cot, fine_out, grad_out, pooled_out,
                f_ps, f_pr, f_prt, c_ps, c_pr, c_pt, p_p, p_t, halo_in, halo_out, f_x, c_x, hid, slope_f, slope_c, g_hl,
                f_high, f_agg, f_norm, f_scale, c_cur, c_high, c_agg, c_norm, c_scale, f_mid, counts, ups, work,
                sb0, sb1, sb2, sb3, ra0, ra1, ra2, ra3, rb0, rb1, rb2, rb3, rc0, rc1, rc2, rc3,
                halo_send, halo_recv, rs_send, rs_recv, ex_send, ex_recv, ag_send, ag_recv):
    sb, ra, rb, rc = (sb0, sb1, sb2, sb3), (ra0, ra1, ra2, ra3), (rb0, rb1, rb2, rb3), (rc0, rc1, rc2, rc3)
    gx, gy = lax.axis_index("gx"), lax.axis_index("gy")
    nf, ef = fnodes.shape[2], fedges.shape[3]
    nc, ec = c_cur.shape[1], cedges.shape[3]
    width = halo_in.shape[2]
    span = 4 * width
    x_peers = [lax.rem(gx + d, nx) for d in range(1, nx)]
    y_peers = [lax.rem(gy + d, ny) for d in range(1, ny)]

    barrier = pltpu.get_barrier_semaphore()
    for peer in x_peers:
        pl.semaphore_signal(barrier, inc=1, device_id=(peer, gy), device_id_type=MESH)
    for peer in y_peers:
        pl.semaphore_signal(barrier, inc=1, device_id=(gx, peer), device_id_type=MESH)

    lane = lax.broadcasted_iota(jnp.int32, (LANES, LANES), 1)
    sub = lax.broadcasted_iota(jnp.int32, (LANES, LANES), 0)

    def edge_row(edges, row, start, live):
        picked = edges[0, 0, pl.ds(row, 1), pl.ds(start, LANES)]
        wide = jnp.broadcast_to(picked, (LANES, LANES))
        if live is not None:
            wide = jnp.where(lane + start < live, wide, -1)
        return wide

    def mark_rows(dst, wide, start, count):
        offsets = wide.T - lane
        for c in range(count // LANES):
            dst[pl.ds(start, LANES), pl.ds(c * LANES, LANES)] = marks(offsets, c * LANES)

    def mark_cols(dst, base, wide, start, count):
        offsets = wide - sub
        for c in range(count // LANES):
            dst[pl.ds(base + c * LANES, LANES), pl.ds(start, LANES)] = marks(offsets, c * LANES)

    has = (gx > 0, gx < nx - 1, gy > 0, gy < ny - 1)
    place = ((gx - 1, gy), (gx + 1, gy), (gx, gy - 1), (gx, gy + 1))
    far = (1, 0, 3, 2)

    def halo_copy(turn, d):
        return pltpu.make_async_remote_copy(
            src_ref=halo_out.at[turn, d], dst_ref=halo_in.at[turn, pl.ds(far[d] * width, width)],
            send_sem=halo_send.at[turn, d], recv_sem=halo_recv.at[turn, far[d]],
            device_id=place[d], device_id_type=MESH)

    def halo_start(turn):
        for d in range(4):
            @pl.when(has[d])
            def _(d=d):
                halo_copy(turn, d).start()

    def halo_wait(turn):
        for d in range(4):
            @pl.when(has[d])
            def _(d=d):
                pltpu.make_async_remote_copy(
                    src_ref=halo_out.at[turn, d], dst_ref=halo_in.at[turn, pl.ds(d * width, width)],
                    send_sem=halo_send.at[turn, d], recv_sem=halo_recv.at[turn, d],
                    device_id=place[d], device_id_type=MESH).wait_recv()

    def halo_flush(turn):
        for d in range(4):
            @pl.when(has[d])
            def _(d=d):
                halo_copy(turn, d).wait_send()

    def is_block(target, b):
        return jnp.where(target == b, 1.0, 0.0)

    def pick_block(turn, d, m, target, blocks):
        total = blocks[0].astype(F32) * is_block(target, 0)
        for b in range(1, len(blocks)):
            total = total + blocks[b].astype(F32) * is_block(target, b)
        halo_out[turn, d, m * BLOCK:(m + 1) * BLOCK, :] = total.astype(BF)

    chunk = [rows // nx for rows in group_rows]

    def rs_copies(g):
        return [pltpu.make_async_remote_copy(
            src_ref=sb[g].at[pl.ds(pl.multiple_of(peer * chunk[g], 16), chunk[g])], dst_ref=ra[g].at[d],
            send_sem=rs_send.at[g, d], recv_sem=rs_recv.at[g, d],
            device_id=(peer, gy), device_id_type=MESH) for d, peer in enumerate(x_peers)]

    def ex_copies(g):
        return [pltpu.make_async_remote_copy(
            src_ref=rb[g].at[gy], dst_ref=rb[g].at[gy], send_sem=ex_send.at[g, d], recv_sem=ex_recv.at[g, d],
            device_id=(gx, peer), device_id_type=MESH) for d, peer in enumerate(y_peers)]

    def ag_copies(g):
        return [pltpu.make_async_remote_copy(
            src_ref=rc[g].at[gx], dst_ref=rc[g].at[gx], send_sem=ag_send.at[g, d], recv_sem=ag_recv.at[g, d],
            device_id=(peer, gy), device_id_type=MESH) for d, peer in enumerate(x_peers)]

    def put_terms(g, blocks, vectors):
        rows = 0
        for block in blocks:
            sb[g][rows:rows + LANES, :] = block.astype(BF)
            rows += LANES
        rest = group_rows[g] - rows
        lines = jnp.concatenate(vectors + [jnp.zeros((16 - len(vectors), LANES), F32)], axis=0)
        sb[g][rows:rows + 16, :] = lines.astype(BF)
        if rest > 16:
            sb[g][rows + 16:, :] = jnp.zeros((rest - 16, LANES), BF)

    def sum_first(g):
        for copy in rs_copies(g):
            copy.start()

    def sum_second(g):
        for copy in rs_copies(g):
            copy.wait_recv()
        total = sb[g][pl.ds(pl.multiple_of(gx * chunk[g], 16), chunk[g]), :].astype(F32)
        for d in range(nx - 1):
            total = total + ra[g][d].astype(F32)
        rb[g][gy] = total.astype(BF)
        for copy in ex_copies(g):
            copy.start()

    def sum_third(g):
        for copy in ex_copies(g):
            copy.wait_recv()
        total = rb[g][0].astype(F32)
        for j in range(1, ny):
            total = total + rb[g][j].astype(F32)
        rc[g][gx] = total.astype(BF)
        for copy in ag_copies(g):
            copy.start()

    def sum_fourth(g, start):
        for copy in ag_copies(g):
            copy.wait_recv()
        for i in range(nx):
            grad_out[start + i * chunk[g]:start + (i + 1) * chunk[g], :] = rc[g][i]

    def sum_flush(g):
        for copy in rs_copies(g) + ex_copies(g) + ag_copies(g):
            copy.wait_send()

    live = flive[0, 0]
    for d in range(4):
        for m in range(width // BLOCK):
            pick_block(0, d, m, fhalo_list[0, 0, d, m], [fnodes[0, 0, n:n + BLOCK, :] for n in range(0, nf, BLOCK)])
    for turn in range(5):
        for d in range(4):
            @pl.when(jnp.logical_not(has[d]))
            def _(turn=turn, d=d):
                halo_in[turn, pl.ds(d * width, width), :] = jnp.zeros((width, LANES), BF)

    pl.semaphore_wait(barrier, nx + ny - 2)
    halo_start(0)

    @pl.loop(0, ef // LANES)
    def _(i):
        start = pl.multiple_of(i * LANES, LANES)
        senders = edge_row(fedges, 0, start, live)
        receivers = edge_row(fedges, 1, start, live)
        mark_rows(f_ps, senders, start, nf + span)
        mark_rows(f_pr, receivers, start, nf)
        mark_cols(f_prt, 0, receivers, start, nf)

    @pl.loop(0, nf // LANES)
    def _(i):
        start = pl.multiple_of(i * LANES, LANES)
        picked = pool[0, 0:1, pl.ds(start, LANES)]
        wide = jnp.broadcast_to(picked[0:1], (LANES, LANES))
        mark_rows(p_p, wide, start, nc)
        mark_cols(p_t, 0, wide, start, nc)

    seed = dot(p_t[...], side(cot[0, 0], jnp.ones((nf, LANES), BF)))
    ups[...] = seed[:, :LANES] * loss_scale
    counts[...] = seed[:, LANES:]

    def pick_own(ps, pr, x, rows_of, count, edges):
        @pl.loop(0, edges // ROWS)
        def _(i):
            rows = pl.ds(pl.multiple_of(i * ROWS, ROWS), ROWS)
            own = rows_of()
            x[rows, 0:LANES] = dot(ps[rows, 0:count], own).astype(BF)
            x[rows, LANES:2 * LANES] = dot(pr[rows, :], own).astype(BF)

    def activate(ps, x, halo, count, w01, bias, slope, edges):
        @pl.loop(0, edges // ROWS)
        def _(i):
            rows = pl.ds(pl.multiple_of(i * ROWS, ROWS), ROWS)
            more = dot(ps[rows, count:count + span], halo())
            both = side((x[rows, 0:LANES].astype(F32) + more).astype(BF), x[rows, LANES:2 * LANES])
            x[rows, 0:LANES] = both[:, :LANES]
            pre = dot(both, w01) + bias
            gate = jax.nn.sigmoid(pre)
            hid[rows, :] = (pre * gate).astype(BF)
            slope[rows, :] = gate * (1.0 + pre * (1.0 - gate))

    def weight(w, k):
        return w[k]

    def pair(w, k):
        return jnp.concatenate([weight(w, k), weight(w, k + 1)], axis=0)

    def settle(rows_of, prt, high_ref, agg_ref, norm_ref, scale_ref, w, gain, edges):
        high, low = parts(dot(prt, hid[0:edges, :]))
        w2 = weight(w, 2)
        agg = dot(side(high, low), jnp.concatenate([w2, w2], axis=0)).astype(BF)
        own = rows_of()
        normed, scale = norm(dot(side(own, agg), pair(w, 3)))
        high_ref[...] = high
        agg_ref[...] = agg
        norm_ref[...] = normed
        scale_ref[...] = jnp.broadcast_to(scale, normed.shape)
        return (own.astype(F32) + gain * normed).astype(BF)

    def fine_rows():
        return fnodes[0, 0]

    pick_own(f_ps, f_pr, f_x, fine_rows, nf, ef)
    halo_wait(0)
    activate(f_ps, f_x, lambda: halo_in[0], nf, pair(fw, 0), fb[...][None, :], slope_f, ef)
    mid = settle(fine_rows, f_prt[...], f_high, f_agg, f_norm, f_scale, fw, fg[...][None, :], ef)
    f_mid[...] = mid

    c_cur[0] = (dot(p_t[...], mid) / counts[...]).astype(BF)

    def coarse_send(k):
        for d in range(4):
            for m in range(width // BLOCK):
                pick_block(1 + k, d, m, chalo_list[0, 0, d, m], [c_cur[k, n:n + BLOCK, :] for n in range(0, nc, BLOCK)])
        halo_start(1 + k)

    coarse_send(0)

    @pl.loop(0, ec // LANES)
    def _(i):
        start = pl.multiple_of(i * LANES, LANES)
        senders = edge_row(cedges, 0, start, None)
        receivers = edge_row(cedges, 1, start, None)
        mark_rows(c_ps, senders, start, nc + span)
        mark_rows(c_pr, receivers, start, nc)
        mark_cols(c_pt, 0, senders, start, nc + span)
        mark_cols(c_pt, nc + span, receivers, start, nc)

    steps = cw.shape[0]
    for k in range(steps):
        def rows_of(k=k):
            return c_cur[k]

        pick_own(c_ps, c_pr, c_x, rows_of, nc, ec)
        halo_wait(1 + k)
        activate(c_ps, c_x, lambda k=k: halo_in[1 + k], nc, pair(cw.at[k], 0), cb[k:k + 1, :], slope_c.at[k], ec)
        after = settle(rows_of, c_pt[nc + span:, :], c_high.at[k], c_agg.at[k], c_norm.at[k], c_scale.at[k], cw.at[k],
                       cg[k:k + 1, :], ec)
        c_cur[k + 1] = after
        if k + 1 < steps:
            coarse_send(k + 1)

    def back_nodes(up, norm_ref, scale_ref, w, gain):
        normed = norm_ref[...]
        grad_gain = jnp.sum(up * normed, axis=0, keepdims=True)
        grad_pre = norm_back(up * gain, normed, scale_ref[...])
        grad_agg = times_t(grad_pre, weight(w, 4))
        grad_hidden = times_t(grad_agg, weight(w, 2))
        return grad_gain, grad_pre, grad_agg, side(*parts(grad_hidden))

    def back_edges(pr, hidden_parts, slope, edges):
        work[0:hidden_parts.shape[0], :] = hidden_parts
        count = hidden_parts.shape[0]

        def one(i, total):
            rows = pl.ds(pl.multiple_of(i * ROWS, ROWS), ROWS)
            grad = halves(dot(pr[rows, :], work[0:count, :])) * slope[rows, :]
            g_hl[rows, :] = side(*parts(grad))
            return total + jnp.sum(grad.reshape(ROWS // 8, 8, LANES), axis=0)

        return jnp.sum(lax.fori_loop(0, edges // ROWS, one, jnp.zeros((8, LANES), F32)), axis=0, keepdims=True)

    def node_terms(own, agg, high, grad_pre, grad_agg):
        last = halves_of(dot_rows(side(own, agg), side(*parts(grad_pre))))
        message = halves(dot_rows(high, side(*parts(grad_agg))))
        return message, last[:LANES], last[LANES:]

    def halves_of(values):
        return values[:, :LANES] + values[:, LANES:]

    c_groups = [None] * steps
    for k in reversed(range(steps)):
        turn = 3 + (steps - 1 - k)
        g = steps - 1 - k
        w = cw.at[k]
        up = ups[...]
        grad_gain, grad_pre, grad_agg, hidden_parts = back_nodes(up, c_norm.at[k], c_scale.at[k], w, cg[k:k + 1, :])
        grad_bias = back_edges(c_pr, hidden_parts, slope_c.at[k], ec)
        far_send = halves(dot(c_pt[nc:nc + span, :], g_hl[...]))
        far_grad = times_t(far_send, weight(w, 0)).astype(BF)
        for d in range(4):
            halo_out[turn, d] = far_grad[d * width:(d + 1) * width]
        halo_start(turn)
        own_send = halves(dot(c_pt[0:nc, :], g_hl[...]))
        own_recv = halves(dot(c_pt[nc + span:, :], g_hl[...]))
        own = c_cur[k]
        nodes_grad = up + dot_t(
            side(*parts(grad_pre), *parts(own_recv), *parts(own_send)),
            side(weight(w, 3), weight(w, 3), weight(w, 1), weight(w, 1), weight(w, 0), weight(w, 0)))
        sender = halves(dot_rows(own, side(*parts(own_send)))) + halves(dot_rows(halo_in[1 + k], side(*parts(far_send))))
        receiver = halves(dot_rows(own, side(*parts(own_recv))))
        message, self_term, agg_term = node_terms(own, c_agg[k], c_high[k], grad_pre, grad_agg)
        put_terms(g, [sender, receiver, message, self_term, agg_term], [grad_bias, grad_gain])
        sum_first(g)
        if g == 0:
            lifted = dot(p_p[...], c_cur[steps])
            fine_out[...] = (f_mid[...].astype(F32) + lifted).astype(BF)
        else:
            sum_second(g - 1)
        halo_wait(turn)
        blocks = [nodes_grad[b * BLOCK:(b + 1) * BLOCK] for b in range(nc // BLOCK)]
        for d in range(4):
            for m in range(width // BLOCK):
                target = chalo_list[0, 0, d, m]
                back = halo_in[turn, pl.ds(d * width + m * BLOCK, BLOCK), :].astype(F32)
                blocks = [block + back * is_block(target, b) for b, block in enumerate(blocks)]
        ups[...] = jnp.concatenate(blocks, axis=0)

    up = ups[...]
    pooled_out[...] = up * out_scale
    spread = up / counts[...]
    fine_up = cot[0, 0].astype(F32) * loss_scale + halves(dot(p_p[...], side(*parts(spread))))
    grad_gain, grad_pre, grad_agg, hidden_parts = back_nodes(fine_up, f_norm, f_scale, fw, fg[...][None, :])
    message, self_term, agg_term = node_terms(fine_rows(), f_agg[...], f_high[...], grad_pre, grad_agg)
    put_terms(2, [message, self_term, agg_term], [grad_gain])
    sum_first(2)
    grad_bias = back_edges(f_pr, hidden_parts, slope_f, ef)
    ends = halves_of(dot_rows(f_x[...], g_hl[0:ef, :]))
    put_terms(3, [ends[:LANES], ends[LANES:]], [grad_bias])
    sum_first(3)
    sum_third(0)
    sum_second(1)
    sum_second(2)
    sum_second(3)
    starts = [sum(group_rows[:g]) for g in range(4)]
    sum_third(1)
    sum_third(2)
    sum_third(3)
    for g in range(4):
        sum_fourth(g, starts[g])
    for turn in range(5):
        halo_flush(turn)
    for g in range(4):
        sum_flush(g)


def finish_kernel(group_rows, fine_in, grads, pooled_in, fine_out, gfw, gfb, gfg, gcw, gcb, gcg, pooled_out):
    fine_out[0, 0] = fine_in[...]
    pooled_out[0, 0] = pooled_in[...]
    starts = [sum(group_rows[:g]) for g in range(4)]

    def block(start):
        return grads[start:start + LANES, :].astype(F32)

    def lines(start):
        return grads[start:start + 16, :].astype(F32)

    steps = gcw.shape[0]
    for k in range(steps):
        start = starts[steps - 1 - k]
        for n in range(5):
            gcw[k, n] = block(start + n * LANES)
        tail = lines(start + 5 * LANES)
        gcb[k:k + 1, :] = tail[0:1]
        gcg[k:k + 1, :] = tail[1:2]
    for n in range(2):
        gfw[n] = block(starts[3] + n * LANES)
    for n in range(3):
        gfw[2 + n] = block(starts[2] + n * LANES)
    gfb[...] = lines(starts[3] + 2 * LANES)[0]
    gfg[...] = lines(starts[2] + 3 * LANES)[0]


def body(nx, ny, fine_nodes, fine_edges, fine_live, fine_halo, pool_map, coarse_edges, coarse_halo,
         fine_weights, fine_bias, fine_gain, coarse_weights, coarse_bias, coarse_gain, cotangent):
    nf, h = fine_nodes.shape[2:]
    ef, ec = fine_edges.shape[3], coarse_edges.shape[3]
    nc = NC_DEV
    steps = coarse_weights.shape[0]
    fw_span = 4 * fine_halo.shape[3] * BLOCK
    cw_span = 4 * coarse_halo.shape[3] * BLOCK
    width = fw_span // 4
    assert fw_span == cw_span and h == LANES and steps == 2
    loss_scale = 1.0 / math.sqrt(nf * nx * ny)
    out_scale = math.sqrt(nf * nx * ny)
    unit = nx * 16
    group_rows = tuple(round_up(r + 16, unit) for r in (5 * h, 5 * h, 3 * h, 2 * h))
    vmem = pl.BlockSpec(memory_space=pltpu.VMEM)
    smem = pl.BlockSpec(memory_space=pltpu.SMEM)
    scratch = [
        pltpu.VMEM((ef, nf + fw_span), BF), pltpu.VMEM((ef, nf), BF), pltpu.VMEM((nf, ef), BF),
        pltpu.VMEM((ec, nc + cw_span), BF), pltpu.VMEM((ec, nc), BF), pltpu.VMEM((nc + cw_span + nc, ec), BF),
        pltpu.VMEM((nf, nc), BF), pltpu.VMEM((nc, nf), BF),
        pltpu.VMEM((5, 4 * width, h), BF), pltpu.VMEM((5, 4, width, h), BF),
        pltpu.VMEM((ef, 2 * h), BF), pltpu.VMEM((ec, 2 * h), BF), pltpu.VMEM((max(ef, ec), h), BF),
        pltpu.VMEM((ef, h), F32), pltpu.VMEM((steps, ec, h), F32), pltpu.VMEM((max(ef, ec), 2 * h), BF),
        pltpu.VMEM((nf, h), BF), pltpu.VMEM((nf, h), BF), pltpu.VMEM((nf, h), F32), pltpu.VMEM((nf, h), F32),
        pltpu.VMEM((steps + 1, nc, h), BF), pltpu.VMEM((steps, nc, h), BF), pltpu.VMEM((steps, nc, h), BF),
        pltpu.VMEM((steps, nc, h), F32), pltpu.VMEM((steps, nc, h), F32),
        pltpu.VMEM((nf, h), BF), pltpu.VMEM((nc, h), F32), pltpu.VMEM((nc, h), F32), pltpu.VMEM((max(nf, nc), 2 * h), BF),
    ]
    scratch += [pltpu.VMEM((r, h), BF) for r in group_rows]
    scratch += [pltpu.VMEM((nx - 1, r // nx, h), BF) for r in group_rows]
    scratch += [pltpu.VMEM((ny, r // nx, h), BF) for r in group_rows]
    scratch += [pltpu.VMEM((nx, r // nx, h), BF) for r in group_rows]
    dma = pltpu.SemaphoreType.DMA
    scratch += [dma((5, 4)), dma((5, 4)), dma((4, nx - 1)), dma((4, nx - 1)), dma((4, ny - 1)), dma((4, ny - 1)),
                dma((4, nx - 1)), dma((4, nx - 1))]
    fine_mid, grads, pooled = pl.pallas_call(
        functools.partial(step_kernel, nx, ny, loss_scale, out_scale, group_rows),
        out_shape=(jax.ShapeDtypeStruct((nf, h), BF), jax.ShapeDtypeStruct((sum(group_rows), h), BF),
                   jax.ShapeDtypeStruct((nc, h), F32)),
        in_specs=[vmem, vmem, smem, smem, vmem, vmem, smem, vmem, vmem, vmem, vmem, vmem, vmem, vmem],
        out_specs=(vmem, vmem, vmem),
        scratch_shapes=scratch,
        compiler_params=pltpu.CompilerParams(collective_id=0, has_side_effects=True, vmem_limit_bytes=48 * 1024 * 1024),
        name="step",
    )(fine_nodes, fine_edges, fine_live, fine_halo, pool_map, coarse_edges, coarse_halo,
      fine_weights, fine_bias, fine_gain, coarse_weights, coarse_bias, coarse_gain, cotangent)
    return pl.pallas_call(
        functools.partial(finish_kernel, group_rows),
        out_shape=(jax.ShapeDtypeStruct((1, 1, nf, h), BF), jax.ShapeDtypeStruct(fine_weights.shape, F32),
                   jax.ShapeDtypeStruct(fine_bias.shape, F32), jax.ShapeDtypeStruct(fine_gain.shape, F32),
                   jax.ShapeDtypeStruct(coarse_weights.shape, F32), jax.ShapeDtypeStruct(coarse_bias.shape, F32),
                   jax.ShapeDtypeStruct(coarse_gain.shape, F32), jax.ShapeDtypeStruct((1, 1, nc, h), F32)),
        in_specs=[vmem] * 3,
        out_specs=(vmem,) * 8,
        name="finish",
    )(fine_mid, grads, pooled)


def solution(mesh):
    grid = P("gx", "gy")
    return jax.shard_map(
        functools.partial(body, mesh.shape["gx"], mesh.shape["gy"]),
        mesh=mesh,
        in_specs=(grid, grid, grid, grid, grid, grid, grid, P(), P(), P(), P(), P(), P(), grid),
        out_specs=(grid, P(), P(), P(), P(), P(), P(), grid),
        check_vma=False,
    )
```

time: 308 us -> 78.3 us (0.25)
  waiting for transfers between devices: 101 us -> 0 us
  Pallas kernels: 0 us -> 67.4 us
  starting transfers between devices: 53.6 us -> 0 us
  matrix products: 49.7 us -> 0 us
  blocking collectives: 45 us -> 0 us
  other arithmetic: 17.3 us -> 0 us
  local copies, waits for them, and re-layouts: 23.3 us -> 8.03 us
  between operations: 16.3 us -> 1.37 us
    psum x1 -> x0, waiting for transfers between devices: 88.4 us -> none  [body(): lax.psum((fine_terms[0], fine_terms[1], fine_terms[2], coarse_stacked[0],...]
    pallas_call x0 -> x2, Pallas kernels: none -> 67.4 us  [the longest x1 65.2 us: body(): pl.pallas_call(functools.partial(step_kernel, nx, ny, loss_scale, out_sca...]
    ppermute x20 -> x0, starting transfers between devices: 53.5 us -> none  [the longest x10 40.1 us: extended_2(): before = lax.ppermute(last, axis, up)]
    dot_general x85 -> x0, matrix products: 49.7 us -> none  [the longest x7 17.1 us: dot_rows(): lax.dot_general(left, right, (((0,), (0,)), ((), ())), preferred_element_...]
    psum x1 -> x0, blocking collectives: 45 us -> none  [body(): lax.psum((fine_terms[0], fine_terms[1], fine_terms[2], coarse_stacked[0],...]
    ppermute x20 -> x0, waiting for transfers between devices: 13 us -> none  [the longest x10 12.7 us: extended_2(): after = lax.ppermute(initial, axis, down)]
    unnamed x143 -> x34, local copies, waits for them, and re-layouts: 14.2 us -> 8.03 us
    eq x4 -> x0, other arithmetic: 4.92 us -> none  [make_one_hot(): pool_rows[:, None] == lax.iota(jnp.int32, coarse_count)[None, :]]
  transfers between devices with their start and end apart: 21 -> 0, of which waited for: 6 -> 0; matrix products, arithmetic and copies ran while one was open for 8% -> 0% of each run, Pallas kernels for 0% -> 0%
where the time goes in v1:
time: 78.3 us; the launch traced here: 76.8 us
  Pallas kernels  67.4 us (86%)
  local copies, waits for them, and re-layouts  8.03 us (10%)
  between operations  1.37 us (2%)
    pallas_call x1, Pallas kernels, body(): pl.pallas_call(functools.partial(step_kernel, nx, ny, loss_scale, out_sca...  65.2 us
    unnamed x34, local copies, waits for them, and re-layouts  8.03 us
    pallas_call x1, Pallas kernels, body(): pl.pallas_call(functools.partial(finish_kernel, group_rows), out_shape=(j...  2.18 us

profile of v1, /device:TPU:0, one launch (start us, length us, event | category | flops | bytes accessed | tf_op | source)
XLA Modules:
  0.0 76.8 jit_solution(8306642266404572507)
XLA Ops:
  0.6 0.0 copy-start.14
  0.6 0.0 copy-start.15
  1.3 0.0 copy-done.14
  1.3 0.0 copy-start.9
  1.3 0.0 copy-start.13
  1.3 0.1 copy.22.fhalo_list
  1.4 0.0 copy-done.15
  1.4 0.0 copy-start.10
  1.4 0.0 copy-start.11
  1.4 0.0 copy-start.12
  1.5 0.1 copy.23.chalo_list
  1.5 0.5 copy-done.9
  2.0 0.0 copy-done.13
  2.0 0.1 copy-done.10
  2.1 0.0 copy-done.11
  2.1 0.0 copy-done.12
  2.1 0.0 copy-start.1
  2.1 1.0 %copy-done.1 = bf16[2,5,128,128]{3,2,1,0:T(8,128)(2,1)S(1)} copy-done((bf16[2,5,128,128]{3,2,1,0:T(8,128)(2,1)S(1)}, bf16[2,5,128,128]{3,2,1,0:T(8,128)(2,1)}, u32[]{:S(2)}) %copy-start.1) | copy-done | bytes 327704
  3.1 0.0 copy-start.2
  3.1 0.9 %copy-done.2 = bf16[5,128,128]{2,1,0:T(8,128)(2,1)S(1)} copy-done((bf16[5,128,128]{2,1,0:T(8,128)(2,1)S(1)}, bf16[5,128,128]{2,1,0:T(8,128)(2,1)}, u32[]{:S(2)}) %copy-start.2) | copy-done | bytes 163864
  4.0 0.0 copy-start.5
  4.0 0.9 %copy-done.5 = bf16[1,1,512,128]{3,2,1,0:T(8,128)(2,1)S(1)} copy-done((bf16[1,1,512,128]{3,2,1,0:T(8,128)(2,1)S(1)}, bf16[1,1,512,128]{3,2,1,0:T(8,128)(2,1)}, u32[]{:S(2)}) %copy-start.5) | copy-done | bytes 131096
  4.9 0.0 copy-start.6
  4.9 0.9 %copy-done.6 = bf16[1,1,512,128]{3,2,1,0:T(8,128)(2,1)S(1)} copy-done((bf16[1,1,512,128]{3,2,1,0:T(8,128)(2,1)S(1)}, bf16[1,1,512,128]{3,2,1,0:T(8,128)(2,1)}, u32[]{:S(2)}) %copy-start.6) | copy-done | bytes 131096
  5.8 0.0 copy-start.7
  5.8 0.7 copy-done.7
  6.6 0.0 copy-start.8
  6.6 0.7 copy-done.8
  7.3 65.2 %step.1 = (bf16[512,128]{1,0:T(8,128)(2,1)S(1)}, bf16[2176,128]{1,0:T(8,128)(2,1)S(1)}, f32[256,128]{1,0:T(8,128)S(1)}) custom-call(bf16[1,1,512,128]{3,2,1,0:T(8,128)(2,1)S(1)} %copy-done.5, s32[1,1,2,1536]{3,2,1,0:T(2,128)S(1)} %copy-done.8, s32[1,1]{1,0:T(1,128)S(6)} %copy.24.flive, s32[1,1,4,1]{3,2,1,0:T(4,128)S(1)} %copy.22.fhalo_list, ...), custom_call_target="tpu_custom_call" | custom-call | tf_op jit(solution)/shard_map/step/pallas_call | solution.py:488
  72.5 0.0 copy-start
  72.5 0.8 %copy-done = bf16[2176,128]{1,0:T(8,128)(2,1)} copy-done((bf16[2176,128]{1,0:T(8,128)(2,1)}, bf16[2176,128]{1,0:T(8,128)(2,1)S(1)}, u32[]{:S(2)}) %copy-start) | copy-done | bytes 557080
  73.3 0.0 copy-start.3
  73.3 0.6 copy-done.3
  74.0 0.0 copy-start.4
  74.0 0.7 copy-done.4
  74.6 2.2 %finish.1 = (bf16[1,1,512,128]{3,2,1,0:T(8,128)(2,1)}, f32[5,128,128]{2,1,0:T(8,128)}, f32[128]{0:T(128)}, f32[128]{0:T(128)}, f32[2,5,128,128]{3,2,1,0:T(8,128)...) custom-call(bf16[512,128]{1,0:T(8,128)(2,1)} %copy-done.3, bf16[2176,128]{1,0:T(8,128)(2,1)} %copy-done, ...), custom_call_target="tpu_custom_call" | custom-call | tf_op jit(solution)/shard_map/finish/pallas_call | solution.py:499
Async XLA Ops:
  0.6 0.7 copy-start.14
  0.6 0.8 %copy-start.15 = (s32[1,1,4,1]{2,3,1,0:T(1,128)S(1)}, s32[1,1,4,1]{2,3,1,0:T(1,128)}, u32[]{:S(2)}) copy-start(s32[1,1,4,1]{2,3,1,0:T(1,128)} %param.20) | copy-start | bytes 52
  1.3 0.7 copy-start.9
  1.3 0.7 copy-start.13
  1.4 0.7 copy-start.10
  1.4 0.7 copy-start.11
  1.4 0.7 copy-start.12
  2.1 1.0 %copy-start.1 = (bf16[2,5,128,128]{3,2,1,0:T(8,128)(2,1)S(1)}, bf16[2,5,128,128]{3,2,1,0:T(8,128)(2,1)}, u32[]{:S(2)}) copy-start(bf16[2,5,128,128]{3,2,1,0:T(8,128)(2,1)} %cw.1) | copy-start | bytes 983044
  3.1 0.9 %copy-start.2 = (bf16[5,128,128]{2,1,0:T(8,128)(2,1)S(1)}, bf16[5,128,128]{2,1,0:T(8,128)(2,1)}, u32[]{:S(2)}) copy-start(bf16[5,128,128]{2,1,0:T(8,128)(2,1)} %fw.1) | copy-start | bytes 491524
  4.0 0.9 %copy-start.5 = (bf16[1,1,512,128]{3,2,1,0:T(8,128)(2,1)S(1)}, bf16[1,1,512,128]{3,2,1,0:T(8,128)(2,1)}, u32[]{:S(2)}) copy-start(bf16[1,1,512,128]{3,2,1,0:T(8,128)(2,1)} %fnodes.1) | copy-start | bytes 393220
  4.9 0.9 %copy-start.6 = (bf16[1,1,512,128]{3,2,1,0:T(8,128)(2,1)S(1)}, bf16[1,1,512,128]{3,2,1,0:T(8,128)(2,1)}, u32[]{:S(2)}) copy-start(bf16[1,1,512,128]{3,2,1,0:T(8,128)(2,1)} %cot.1) | copy-start | bytes 393220
  5.8 0.7 copy-start.7
  6.6 0.7 copy-start.8
  72.5 0.8 %copy-start = (bf16[2176,128]{1,0:T(8,128)(2,1)}, bf16[2176,128]{1,0:T(8,128)(2,1)S(1)}, u32[]{:S(2)}) copy-start(bf16[2176,128]{1,0:T(8,128)(2,1)S(1)} %get-tuple-element.12.grads) | copy-start | bytes 1671172
  73.3 0.6 copy-start.3
  74.0 0.7 copy-start.4
